TPU v7x, 512 devices: a whole 4x8x8 slice. The times are simulated.
512 devices in a mesh: gz: 16 (over z, core), xy: 32 (over y, x).
Axes of the slice: x: 4, y: 8, z: 8, core: 2. Of those that a mesh axis runs over, the one named last changes fastest.
Arguments:
- positions: float32 [3, 65536], P(None, ('gz', 'xy')), may hold values from 0 to 64, as said below
- velocities: float32 [3, 65536], P(None, ('gz', 'xy')), may hold values from -6 to 6
- forces: float32 [3, 65536], P(None, ('gz', 'xy')), may hold values from -6 to 6
- species: int32 [65536], P(('gz', 'xy')), may hold values from 0 to 3
- counts: int32 [512], P(('gz', 'xy')), may hold values from 16 to 128, as said below
- neighbours: int32 [24, 65536], P(None, ('gz', 'xy')), may hold values from 0 to 320, as said below
- send_inplane: int32 [2, 16384], P(None, ('gz', 'xy')), may hold values from 0 to 127
- send_normal: int32 [2, 32768], P(None, ('gz', 'xy')), may hold values from 0 to 191
- embedding: float32 [4, 128], replicated, may hold values from -6 to 6
- inverse_mass: float32 [4], replicated, may hold values from 0.25 to 1
- radial_weight: float32 [16, 128], replicated, may hold values from -1.5 to 1.5
- mix_weight: float32 [128, 128], replicated, may hold values from -0.5 to 0.5
- self_weight: float32 [128, 128], replicated, may hold values from -0.5 to 0.5
- charge_weight: float32 [128, 128], replicated, may hold values from -0.5 to 0.5
- readout_weight: float32 [128, 128], replicated, may hold values from -0.5 to 0.5
- readout_vector: float32 [128], replicated, may hold values from -0.5 to 0.5
- kernel_filter: float32 [512, 128], replicated, may hold values from 0.2 to 2
Outputs:
- positions_new: float32 [3, 65536], P(None, ('gz', 'xy'))
- velocities_new: float32 [3, 65536], P(None, ('gz', 'xy'))
- forces_new: float32 [3, 65536], P(None, ('gz', 'xy'))
- energy: float32 [], replicated
Inputs may be any that keep to these rules, and one draw needn't show every extreme that they name: `positions`: coordinates of domain (g, p) lie in [2 p, 2 p + 2) x [0, 4) x [2 g, 2 g + 2). `counts`: the first domain is full; filling falls along the slab-normal axis. `neighbours`: slots of the extended list: own 128, then 32 from the lower and 32 from the upper in-plane neighbour, 64 from the lower and 64 from the upper slab-normal neighbour, then the padding slot 320.
All inputs are finite; a program needn't handle non-finite values.
Results may differ from a plain program's by a relative error of at most 0.0003.
Values sent between devices are 32-bit elements; how exact they have to be, the bound alone decides.
A program may use at most 64 MiB of HBM per device.

v0:
```python
import jax
import jax.numpy as jnp
from jax import lax
from jax.sharding import PartitionSpec as P

KGRID = 8


time_step = 0.5
width_x = 2.0
width_y = 4.0
width_z = 2.0
far_away = 1000.0
softening = 0.25
basis_reach = 6.0
envelope_reach = 4.0
highest = lax.Precision.HIGHEST


def padded(cells, sides, width, closed):
    for axis, dim in sides:
        count = lax.axis_size(axis)
        ends = count if closed else count - 1
        head = lax.slice_in_dim(cells, 0, width, axis=dim)
        tail = lax.slice_in_dim(cells, cells.shape[dim] - width, cells.shape[dim], axis=dim)
        cells = jnp.concatenate(
            [
                lax.ppermute(tail, axis, [(i, (i + 1) % count) for i in range(ends)]),
                cells,
                lax.ppermute(head, axis, [((i + 1) % count, i) for i in range(ends)]),
            ],
            axis=dim,
        )
    return cells


def wave_vectors(grid_side, layers, strips):
    wave_index = jnp.arange(grid_side**3)
    along_x = (wave_index // (grid_side * grid_side)).astype(jnp.float32) / (strips * width_x)
    along_y = (wave_index // grid_side % grid_side - grid_side // 2).astype(jnp.float32) / width_y
    along_z = (wave_index % grid_side - grid_side // 2).astype(jnp.float32) / (layers * width_z)
    wave_rows = 2.0 * jnp.pi * jnp.stack([along_x, along_y, along_z], axis=1)
    keeper = (wave_index != grid_side // 2 * grid_side + grid_side // 2).astype(jnp.float32)
    return (wave_rows, keeper)


def local_terms(
    ext_pos,
    ext_kind,
    ext_live,
    neighbour_rows,
    embedding,
    radial_weight,
    mix_weight,
    self_weight,
    readout_weight,
    readout_vector,
    charge_weight,
):
    own_atoms = neighbour_rows.shape[1]
    kind_values = jnp.arange(embedding.shape[0]).astype(jnp.float32)
    one_hot = (ext_kind[:, None] == kind_values[None, :]).astype(jnp.float32)
    embedded = jnp.dot(one_hot, embedding, precision=highest)
    outgoing = jnp.dot(embedded, mix_weight, precision=highest) * ext_live[:, None]
    centre = ext_pos[:, :own_atoms]
    partner = jnp.take(ext_pos, neighbour_rows, axis=1)
    offsets = partner - centre[:, None, :]
    distance = jnp.sqrt(jnp.sum(offsets * offsets, axis=0) + softening)
    basis_count = radial_weight.shape[0]
    spacing = basis_reach / (basis_count - 1)
    centres = spacing * jnp.arange(basis_count).astype(jnp.float32)
    scaled = (distance[None, :, :] - centres[:, None, None]) / spacing
    envelope = 1.0 / (1.0 + (distance / envelope_reach) ** 4)
    radial_basis = jnp.exp(-scaled * scaled) * envelope[None, :, :]
    filters = jnp.einsum("bma,bc->mac", radial_basis, radial_weight, precision=highest)
    gathered = jnp.take(outgoing, neighbour_rows, axis=0)
    message = jnp.sum(filters * gathered, axis=0)
    hidden = jax.nn.silu(jnp.dot(embedded[:own_atoms], self_weight, precision=highest) + message)
    own_live = ext_live[:own_atoms]
    readout = jnp.dot(
        jax.nn.silu(jnp.dot(hidden, readout_weight, precision=highest)),
        readout_vector,
        precision=highest,
    )
    charges = jnp.dot(hidden, charge_weight, precision=highest) * own_live[:, None]
    return (jnp.sum(readout * own_live), charges)


def structure_terms(wave_rows, own_pos, charges):
    phase = jnp.dot(wave_rows, own_pos, precision=highest)
    cosine_sum = jnp.dot(jnp.cos(phase), charges, precision=highest)
    sine_sum = jnp.dot(jnp.sin(phase), charges, precision=highest)
    return (cosine_sum, sine_sum)


def ewald_pullback(wave_rows, pos_block, charge_block, weight_cos, weight_sin):
    phase = jnp.dot(wave_rows, pos_block, precision=highest)
    cosine = jnp.cos(phase)
    sine = jnp.sin(phase)
    charge_grad = jnp.einsum("ka,kc->ac", cosine, weight_cos, precision=highest) + jnp.einsum(
        "ka,kc->ac", sine, weight_sin, precision=highest
    )
    along_cos = jnp.einsum("kc,ac->ka", weight_cos, charge_block, precision=highest)
    along_sin = jnp.einsum("kc,ac->ka", weight_sin, charge_block, precision=highest)
    phase_grad = cosine * along_sin - sine * along_cos
    pos_grad = jnp.einsum("kd,ka->da", wave_rows, phase_grad, precision=highest)
    return (charge_grad, pos_grad)


def inplane_halo(outgoing):
    return padded(outgoing, (("xy", 0),), 1, True)


def normal_halo(outgoing):
    return padded(outgoing, (("gz", 0),), 1, False)


def local(
    positions,
    velocities,
    forces,
    species,
    counts,
    neighbours,
    send_inplane,
    send_normal,
    embedding,
    inverse_mass,
    radial_weight,
    mix_weight,
    self_weight,
    charge_weight,
    readout_weight,
    readout_vector,
    kernel_filter,
):
    own_atoms = positions.shape[1]
    strips = lax.axis_size("xy")
    layers = lax.axis_size("gz")
    all_atoms = own_atoms * strips * layers
    inplane_count = send_inplane.shape[1]
    normal_count = send_normal.shape[1]
    kind_values = jnp.arange(inverse_mass.shape[0])
    mass_factor = jnp.sum(
        (species[None, :] == kind_values[:, None]).astype(jnp.float32) * inverse_mass[:, None],
        axis=0,
    )
    half_velocity = velocities + 0.5 * time_step * forces * mass_factor[None, :]
    moved = positions + time_step * half_velocity
    filled = counts[0]
    own_live = (jnp.arange(own_atoms) < filled).astype(jnp.float32)
    records = jnp.concatenate(
        [moved, species.astype(jnp.float32)[None, :], own_live[None, :]], axis=0
    )
    outgoing = jnp.stack(
        [jnp.take(records, send_inplane[0], axis=1), jnp.take(records, send_inplane[1], axis=1)]
    )
    arrived = inplane_halo(outgoing)
    strip_index = lax.axis_index("xy")
    box_x = strips * width_x
    row_pick = (jnp.arange(5) == 0).astype(jnp.float32)[:, None]
    from_lower = arrived[0] - row_pick * jnp.where(strip_index == 0, box_x, 0.0)
    from_upper = arrived[3] + row_pick * jnp.where(strip_index == strips - 1, box_x, 0.0)
    first_section = jnp.concatenate([records, from_lower, from_upper], axis=1)
    outgoing = jnp.stack(
        [
            jnp.take(first_section, send_normal[0], axis=1),
            jnp.take(first_section, send_normal[1], axis=1),
        ]
    )
    arrived = normal_halo(outgoing)
    padding = jnp.array([far_away, far_away, far_away, 0.0, 0.0], dtype=jnp.float32)[:, None]
    extended = jnp.concatenate([first_section, arrived[0], arrived[3], padding], axis=1)
    ext_kind = extended[3]
    ext_live = extended[4]

    def local_part(ext_pos):
        return local_terms(
            ext_pos,
            ext_kind,
            ext_live,
            neighbours,
            embedding,
            radial_weight,
            mix_weight,
            self_weight,
            readout_weight,
            readout_vector,
            charge_weight,
        )

    (local_sum, charges), pullback = jax.vjp(local_part, extended[:3])
    wave_rows, keeper = wave_vectors(KGRID, layers, strips)
    cosine_sum, sine_sum = structure_terms(wave_rows, moved, charges)
    cosine_sum, sine_sum = lax.psum((cosine_sum, sine_sum), ("gz", "xy"))
    weight_cos = keeper[:, None] * kernel_filter * cosine_sum / all_atoms
    weight_sin = keeper[:, None] * kernel_filter * sine_sum / all_atoms
    ewald_energy = 0.5 * jnp.sum(weight_cos * cosine_sum + weight_sin * sine_sum)
    charge_grad, pos_grad = ewald_pullback(wave_rows, moved, charges, weight_cos, weight_sin)
    ext_grad = pullback((jnp.ones((), jnp.float32), charge_grad))[0]
    split_one = own_atoms + 2 * inplane_count
    returning = jnp.stack(
        [
            ext_grad[:, split_one : split_one + normal_count],
            ext_grad[:, split_one + normal_count : split_one + 2 * normal_count],
        ]
    )
    came_back = normal_halo(returning)
    section_grad = ext_grad[:, :split_one]
    section_grad = (
        section_grad.at[:, send_normal[0]].add(came_back[0]).at[:, send_normal[1]].add(came_back[3])
    )
    returning = jnp.stack(
        [
            section_grad[:, own_atoms : own_atoms + inplane_count],
            section_grad[:, own_atoms + inplane_count : split_one],
        ]
    )
    came_back = inplane_halo(returning)
    own_grad = (
        section_grad[:, :own_atoms]
        .at[:, send_inplane[0]]
        .add(came_back[0])
        .at[:, send_inplane[1]]
        .add(came_back[3])
    )
    forces_new = -(own_grad + pos_grad)
    velocities_new = half_velocity + 0.5 * time_step * forces_new * mass_factor[None, :]
    local_total = lax.psum(local_sum, ("gz", "xy"))
    energy = (local_total + ewald_energy) / all_atoms
    return (moved, velocities_new, forces_new, energy)


def solution(mesh):
    return jax.shard_map(
        local,
        mesh=mesh,
        in_specs=(
            P(None, ("gz", "xy")),
            P(None, ("gz", "xy")),
            P(None, ("gz", "xy")),
            P(("gz", "xy")),
            P(("gz", "xy")),
            P(None, ("gz", "xy")),
            P(None, ("gz", "xy")),
            P(None, ("gz", "xy")),
            P(),
            P(),
            P(),
            P(),
            P(),
            P(),
            P(),
            P(),
            P(),
        ),
        out_specs=(P(None, ("gz", "xy")), P(None, ("gz", "xy")), P(None, ("gz", "xy")), P()),
        check_vma=False,
    )
```

profile of v0, /device:TPU:1, one launch (start us, length us, event | category | flops | bytes accessed | tf_op | source)
XLA Modules:
  0.0 401.5 jit_solution(13458627474499841923)
XLA Ops:
  7.2 0.7 convert_bitcast_fusion
  7.9 0.8 select_reduce_fusion
  8.7 0.7 broadcast_multiply_fusion
  9.4 0.1 copy.77
  9.5 0.8 copy.76
  10.3 0.8 copy.78
  11.8 0.8 compare_and_fusion.3
  12.7 0.6 gather_fusion.3
  13.4 8.1 %collective-permute-start.1 = (f32[1,5,32]{1,2,0:T(8,128)S(1)}, f32[1,5,32]{1,2,0:T(8,128)S(1)}, u32[]{:S(2)}, u32[]{:S(2)}) collective-permute-start(f32[1,5,32]{1,2,0:T(8,128)S(1)} %select_bitcast_fusion.2), channel_id=1, source_target_pairs={{1,0},{2,1},{3,2},{4,3},{5,4},{6,5},{7,6},{8,7},{9,8},{10,9},{11,1... | collective-permute-start | bytes 1928 | tf_op jit(solution)/shard_map/ppermute | solution.py:30
  21.5 0.6 gather_fusion.2
  22.2 1.9 collective-permute-start
  24.1 0.7 broadcast_clamp_fusion
  24.8 0.7 compare_and_fusion
  25.6 0.7 fusion.57
  26.3 0.8 compare_and_fusion.1
  27.0 0.8 fusion.73
  27.8 0.8 fusion.75
  28.6 1.7 fusion.89
  30.4 0.6 gather_fusion.5
  31.1 4.6 %collective-permute-start.3 = (f32[1,5,64]{1,2,0:T(8,128)S(1)}, f32[1,5,64]{1,2,0:T(8,128)S(1)}, u32[]{:S(2)}, u32[]{:S(2)}) collective-permute-start(f32[1,5,64]{1,2,0:T(8,128)S(1)} %select_bitcast_fusion), channel_id=1, source_target_pairs={{32,0},{64,32},{96,64},{128,96},{160,128},{192,160},{224,192},{256... | collective-permute-start | bytes 3848 | tf_op jit(solution)/shard_map/ppermute | solution.py:30
  35.7 0.6 gather_fusion.4
  36.4 3.0 collective-permute-start.2
  39.6 0.7 collective-permute-done.2
  40.5 0.1 copy.85
  40.7 0.3 fusion.19
  41.0 0.4 convolution_multiply_fusion.2
  41.4 10.8 %gather_fusion.1 = f32[3072,128]{1,0:T(8,128)} fusion(f32[321,128]{1,0:T(8,128)S(1)} %convolution_multiply_fusion.2, s32[3072]{0:T(1024)S(1)} %broadcast_clamp_fusion), kind=kCustom, calls=%fused_computation.5 | custom fusion | bytes 3158016 | tf_op jit(solution)/shard_map/jvp(jit(_take))/gather | solution.py:76
  52.3 8.1 %gather_fusion = f32[3072,3]{1,0:T(8,128)S(1)} fusion(f32[3,321]{0,1:T(8,128)S(1)} %copy.85, s32[3072]{0:T(1024)S(1)} %broadcast_clamp_fusion), kind=kCustom, calls=%fused_computation.4 | custom fusion | bytes 86016 | tf_op jit(solution)/shard_map/jvp(jit(_take))/gather | solution.py:66
  60.4 1.1 multiply_reduce_fusion.1
  61.6 0.2 copy-done.4
  61.8 3.2 multiply_reduce_fusion
  65.1 0.2 convolution_add_fusion.1
  65.3 0.2 convolution_multiply_fusion.3
  65.5 1.1 fusion.93
  66.6 1.1 fusion.92
  67.7 0.2 fusion.54
  67.9 0.8 fusion.12
  68.8 0.7 copy.92
  69.4 103.8 %psum.23 = f32[]{:T(128)} all-reduce(f32[]{:T(128)} %fusion.12), channel_id=1, replica_groups=mesh['gz'=16,'xy'=32] {'gz','xy'}, use_global_device_ids=true, to_apply=%region_14.17 | all-reduce | flops 1 | bytes 8 | tf_op jit(solution)/shard_map/psum | solution.py:229
  173.2 171.2 %all-reduce.4.cloned.1.call-done = (f32[512,128]{1,0:T(8,128)}, f32[512,128]{1,0:T(8,128)}) async-done(((f32[512,128]{1,0:T(8,128)}, f32[512,128]{1,0:T(8,128)}), (f32[512,128]{1,0:T(8,128)}, f32[512,128]{1,0:T(8,128)})) %all-reduce.4.cloned.1.call-update) | async-done | bytes 524304 | tf_op jit(solution)/shard_map/psum | solution.py:195
  344.4 1.4 convolution_multiply_fusion.1
  345.9 1.6 fusion.87
  347.5 0.4 fusion.3
  348.0 0.2 fusion.60
  348.2 0.7 fusion.7
  348.9 0.3 fusion.94
  349.2 0.3 fusion.32
  349.5 1.9 multiply_reduce_fusion.2
  351.5 2.4 fusion.88
  353.9 17.7 %scatter_fusion = f32[3,321]{0,1:T(8,128)S(1)} fusion(f32[3,321]{0,1:T(8,128)S(1)} %pad.3, s32[3072]{0:T(1024)S(1)} %fusion.57, f32[3072,3]{1,0:T(8,128)} %bitcast.133), kind=kCustom, calls=%fused_computation.6 | custom fusion | flops 9216 | bytes 122880 | tf_op jit(solution)/shard_map/transpose(jvp(jit(_take)))/scatter-add | solution.py:66
  371.6 3.1 collective-permute-start.4
  374.8 1.9 collective-permute-start.5
  376.7 0.7 add_reduce_fusion
  378.8 1.0 scatter_custom_fusion.1
  379.7 0.3 collective-permute-done.5
  380.0 1.0 scatter_custom_fusion.2
  381.1 2.9 collective-permute-start.6
  384.0 5.7 %collective-permute-start.7 = (f32[1,3,32]{2,1,0:T(4,128)S(1)}, f32[1,3,32]{2,1,0:T(4,128)S(1)}, u32[]{:S(2)}, u32[]{:S(2)}) collective-permute-start(f32[1,3,32]{2,1,0:T(4,128)S(1)} %bitcast.140), channel_id=1, source_target_pairs={{1,0},{2,1},{3,2},{4,3},{5,4},{6,5},{7,6},{8,7},{9,8},{10,9},{11,1... | collective-permute-start | bytes 1160 | tf_op jit(solution)/shard_map/ppermute | solution.py:30
  389.8 0.1 copy.88
  390.1 0.4 collective-permute-done.7
  390.5 0.8 scatter_fusion.1
  391.3 0.8 scatter_fusion.2
  392.2 0.7 copy.93
  392.9 0.7 copy.94
  (79 shorter events, 1.9 us)
Async XLA Ops:
  7.2 33.9 %copy-start = (f32[128,128]{1,0:T(8,128)S(1)}, f32[128,128]{1,0:T(8,128)}, u32[]{:S(2)}) copy-start(f32[128,128]{1,0:T(8,128)} %param.33) | copy-start | bytes 196612
  7.2 33.2 %copy-start.8 = (f32[5,1]{1,0:T(8,128)S(1)}, f32[5,1]{1,0:T(8,128)}, u32[]{:S(2)}) copy-start(f32[5,1]{1,0:T(8,128)} %constant.177) | copy-start | bytes 64
  7.2 33.5 %copy-start.9 = (f32[4,128]{1,0:T(4,128)S(1)}, f32[4,128]{1,0:T(4,128)}, u32[]{:S(2)}) copy-start(f32[4,128]{1,0:T(4,128)} %param.30) | copy-start | bytes 6148
  7.2 337.2 %all-reduce.4.cloned.1.call-start = ((), (), s32[]{:S(2)}) async-start(), calls=%async_computation | async-start | bytes 1048576 | tf_op jit(solution)/shard_map/psum | solution.py:195
  13.4 16.9 %collective-permute-start.1 = (f32[1,5,32]{1,2,0:T(8,128)S(1)}, f32[1,5,32]{1,2,0:T(8,128)S(1)}, u32[]{:S(2)}, u32[]{:S(2)}) collective-permute-start(f32[1,5,32]{1,2,0:T(8,128)S(1)} %select_bitcast_fusion.2), channel_id=1, source_target_pairs={{1,0},{2,1},{3,2},{4,3},{5,4},{6,5},{7,6},{8,7},{9,8},{10,9},{11,1... | collective-permute-start | bytes 1928 | tf_op jit(solution)/shard_map/ppermute | solution.py:30
  22.2 8.2 %collective-permute-start = (f32[1,5,32]{1,2,0:T(8,128)S(1)}, f32[1,5,32]{1,2,0:T(8,128)S(1)}, u32[]{:S(2)}, u32[]{:S(2)}) collective-permute-start(f32[1,5,32]{1,2,0:T(8,128)S(1)} %select_bitcast_fusion.3), channel_id=1, source_target_pairs={{0,1},{1,2},{2,3},{3,4},{4,5},{5,6},{6,7},{7,8},{8,9},{9,10},{10,1... | collective-permute-start | bytes 1928 | tf_op jit(solution)/shard_map/ppermute | solution.py:28
  31.1 8.4 %collective-permute-start.3 = (f32[1,5,64]{1,2,0:T(8,128)S(1)}, f32[1,5,64]{1,2,0:T(8,128)S(1)}, u32[]{:S(2)}, u32[]{:S(2)}) collective-permute-start(f32[1,5,64]{1,2,0:T(8,128)S(1)} %select_bitcast_fusion), channel_id=1, source_target_pairs={{32,0},{64,32},{96,64},{128,96},{160,128},{192,160},{224,192},{256... | collective-permute-start | bytes 3848 | tf_op jit(solution)/shard_map/ppermute | solution.py:30
  36.4 4.0 collective-permute-start.2
  52.3 9.3 %copy-start.11 = (f32[16,128]{1,0:T(8,128)S(1)}, f32[16,128]{1,0:T(8,128)}, u32[]{:S(2)}) copy-start(f32[16,128]{1,0:T(8,128)} %param.32) | copy-start | bytes 24580
  60.4 1.4 copy-start.4
  60.4 4.6 %copy-start.7 = (f32[128,128]{1,0:T(8,128)S(1)}, f32[128,128]{1,0:T(8,128)}, u32[]{:S(2)}) copy-start(f32[128,128]{1,0:T(8,128)} %param.34) | copy-start | bytes 196612
  60.4 4.9 %copy-start.6 = (f32[128,128]{1,0:T(8,128)S(1)}, f32[128,128]{1,0:T(8,128)}, u32[]{:S(2)}) copy-start(f32[128,128]{1,0:T(8,128)} %param.35) | copy-start | bytes 196612
  65.0 2.7 copy-start.10
  65.0 2.9 copy-start.12
  65.1 279.4 %copy-start.1 = (f32[512,128]{1,0:T(8,128)S(1)}, f32[512,128]{1,0:T(8,128)}, u32[]{:S(2)}) copy-start(f32[512,128]{1,0:T(8,128)} %param.38) | copy-start | bytes 786436
  344.4 3.1 copy-start.3
  344.4 3.8 copy-start.2
  347.5 2.0 copy-start.5
  371.6 7.1 %collective-permute-start.4 = (f32[1,3,64]{1,2,0:T(8,128)S(1)}, f32[1,3,64]{1,2,0:T(8,128)S(1)}, u32[]{:S(2)}, u32[]{:S(2)}) collective-permute-start(f32[1,3,64]{1,2,0:T(8,128)S(1)} %get-tuple-element.43), channel_id=1, source_target_pairs={{0,32},{32,64},{64,96},{96,128},{128,160},{160,192},{192,224},{224... | collective-permute-start | bytes 2312 | tf_op jit(solution)/shard_map/ppermute | solution.py:28
  374.8 5.2 %collective-permute-start.5 = (f32[1,3,64]{1,2,0:T(8,128)S(1)}, f32[1,3,64]{1,2,0:T(8,128)S(1)}, u32[]{:S(2)}, u32[]{:S(2)}) collective-permute-start(f32[1,3,64]{1,2,0:T(8,128)S(1)} %get-tuple-element.42), channel_id=1, source_target_pairs={{32,0},{64,32},{96,64},{128,96},{160,128},{192,160},{224,192},{256... | collective-permute-start | bytes 2312 | tf_op jit(solution)/shard_map/ppermute | solution.py:30
  381.1 8.9 %collective-permute-start.6 = (f32[1,3,32]{2,1,0:T(4,128)S(1)}, f32[1,3,32]{2,1,0:T(4,128)S(1)}, u32[]{:S(2)}, u32[]{:S(2)}) collective-permute-start(f32[1,3,32]{2,1,0:T(4,128)S(1)} %bitcast.138), channel_id=1, source_target_pairs={{0,1},{1,2},{2,3},{3,4},{4,5},{5,6},{6,7},{7,8},{8,9},{9,10},{10,1... | collective-permute-start | bytes 1160 | tf_op jit(solution)/shard_map/ppermute | solution.py:28
  384.0 6.4 %collective-permute-start.7 = (f32[1,3,32]{2,1,0:T(4,128)S(1)}, f32[1,3,32]{2,1,0:T(4,128)S(1)}, u32[]{:S(2)}, u32[]{:S(2)}) collective-permute-start(f32[1,3,32]{2,1,0:T(4,128)S(1)} %bitcast.140), channel_id=1, source_target_pairs={{1,0},{2,1},{3,2},{4,3},{5,4},{6,5},{7,6},{8,7},{9,8},{10,9},{11,1... | collective-permute-start | bytes 1160 | tf_op jit(solution)/shard_map/ppermute | solution.py:30
Sparse Core Ops, SparseCore 0:
  67.8 276.5 all-reduce.3
where the time goes:
time: 402 us; the launch traced here: 401 us
  waiting for transfers between devices  173 us (43%)
  blocking collectives  104 us (26%)
  other arithmetic  33.5 us (8%)
  starting transfers between devices  31.2 us (8%)
  local copies, waits for them, and re-layouts  26.5 us (7%)
  between operations  17.7 us (4%)
  matrix products  16.2 us (4%)
    psum x1, waiting for transfers between devices, local(): cosine_sum, sine_sum = lax.psum((cosine_sum, sine_sum), ('gz', 'xy'))  171 us
    psum x1, blocking collectives, local(): local_total = lax.psum(local_sum, ('gz', 'xy'))  104 us
    ppermute x4, starting transfers between devices, padded(): lax.ppermute(head, axis, [((i + 1) % count, i) for i in range(ends)])  20.3 us
    scatter-add x1, other arithmetic, local_terms(): partner = jnp.take(ext_pos, neighbour_rows, axis=1)  17.7 us
    ppermute x4, starting transfers between devices, padded(): lax.ppermute(tail, axis, [(i, (i + 1) % count) for i in range(ends)])  10.9 us
    gather x1, local copies, waits for them, and re-layouts, local_terms(): gathered = jnp.take(outgoing, neighbour_rows, axis=0)  10.8 us
    gather x1, local copies, waits for them, and re-layouts, local_terms(): partner = jnp.take(ext_pos, neighbour_rows, axis=1)  8.11 us
  transfers between devices with their start and end apart: 9, of which 4 were waited for; matrix products, arithmetic and copies ran while one was open for 3% of the time, Pallas kernels for 0%

commit v1 on v0

v1 whole, which is shorter than its diff:
```python
import jax
import jax.numpy as jnp
from jax import lax
from jax.experimental import pallas as pl
from jax.experimental.pallas import tpu as pltpu
from jax.sharding import PartitionSpec as P

MESH = pl.DeviceIdType.MESH
F32 = jnp.float32
BF16 = jnp.bfloat16

KGRID = 8
NX = 4
NY = 8
NZ = 8
N_GZ = 16
N_XY = 32
ATOMS = 65536.0
OWN = 128
NEIGH = 24
NB = 16
SPECIES = 4
SLOTS = 384
HALF = 32
CHUNK = 4
ZERO_TILE = 4
ZERO_ROW = 4

time_step = 0.5
width_x = 2.0
width_y = 4.0
width_z = 2.0
far_away = 1000.0
softening = 0.25
spacing = 6.0 / (NB - 1)
envelope_reach = 4.0

NN = (((1,), (0,)), ((), ()))
NT = (((1,), (1,)), ((), ()))


def split(value):
    high = value.astype(BF16)
    return high, (value - high.astype(F32)).astype(BF16)


def mm(a, b, dims=NN):
    def one(left, right):
        return lax.dot_general(left, right, dims, preferred_element_type=F32)

    return one(a[0], b[0]) + (one(a[0], b[1]) + one(a[1], b[0]))


def iota(shape, dim):
    return lax.broadcasted_iota(jnp.int32, shape, dim)


def sigmoid(value):
    return 1.0 / (1.0 + jnp.exp(-value))


def rows_of(values):
    return jnp.broadcast_to(values, (8, values.shape[1]))


def take(table, index):
    return jnp.take_along_axis(table, index, axis=1, mode="promise_in_bounds")


def kernel(
    counts_ref,
    mass_ref,
    pos_ref,
    vel_ref,
    force_ref,
    kind_ref,
    neigh_ref,
    sendp_ref,
    sendn_ref,
    emb_ref,
    radial_ref,
    mix_ref,
    self_ref,
    charge_ref,
    readout_ref,
    vector_ref,
    filter_ref,
    pos_out,
    vel_out,
    force_out,
    energy_out,
    rec,
    rec_other,
    idx_p,
    idx_n,
    out_p,
    in_p,
    out_n,
    in_n,
    q_out,
    q_in,
    part,
    gather_1,
    swap_2,
    swap_3,
    final,
    grad_out,
    grad_in,
    misc_out,
    misc_in,
    back_n_out,
    back_n_in,
    back_p_out,
    back_p_in,
    slopes,
    units,
    codes,
    trig_q,
    trig_pt,
    hot,
    send_sem,
    recv_sem,
):
    gz = lax.axis_index("gz")
    xy = lax.axis_index("xy")
    core = lax.rem(gz, 2)
    z = lax.div(gz, 2)
    x = lax.rem(xy, NX)
    y = lax.div(xy, NX)

    partner = (gz + 1 - 2 * core, xy)
    z_peers = [(2 * lax.rem(z + d, NZ) + core, xy) for d in range(1, NZ)]
    y_peers = [(gz, NX * lax.rem(y + d, NY) + x) for d in range(1, NY)]
    x_peers = [(gz, NX * y + lax.rem(x + d, NX)) for d in range(1, NX)]
    p_lower = (gz, lax.rem(xy + N_XY - 1, N_XY))
    p_upper = (gz, lax.rem(xy + 1, N_XY))
    g_lower = (lax.rem(gz + N_GZ - 1, N_GZ), xy)
    g_upper = (lax.rem(gz + 1, N_GZ), xy)

    barrier = pltpu.get_barrier_semaphore()
    greeted = [partner, p_lower, p_upper, g_lower, g_upper] + z_peers + y_peers + x_peers
    for device in greeted:
        pl.semaphore_signal(barrier, inc=1, device_id=device, device_id_type=MESH)

    counter = [0]

    def send(src, dst, device):
        slot = counter[0]
        counter[0] += 1
        copy = pltpu.make_async_remote_copy(
            src_ref=src,
            dst_ref=dst,
            send_sem=send_sem.at[slot],
            recv_sem=recv_sem.at[slot],
            device_id=device,
            device_id_type=MESH,
        )
        copy.start()
        return copy

    started = []

    kind = kind_ref[...]
    mass_row = jnp.where(
        kind == 0,
        mass_ref[0],
        jnp.where(kind == 1, mass_ref[1], jnp.where(kind == 2, mass_ref[2], mass_ref[3])),
    )
    half_velocity = vel_ref[...] + (0.5 * time_step) * force_ref[...] * mass_row
    moved = pos_ref[...] + time_step * half_velocity
    pos_out[...] = moved
    lane = iota((8, OWN), 1)
    sub = iota((8, OWN), 0)
    live = (lane < counts_ref[0]).astype(F32)
    rec[...] = jnp.zeros((8, OWN), F32)
    rec[0:3, :] = moved
    rec[3:4, :] = kind.astype(F32)
    rec[4:5, :] = live[0:1, :]
    own = rec[...]

    idx_p[...] = jnp.zeros((1, OWN), jnp.int32)
    idx_p[0:1, 0:32] = sendp_ref[1:2, :]
    idx_p[0:1, 32:64] = sendp_ref[0:1, :]
    idx_n[0:1, 0:64] = sendn_ref[0:1, :]
    idx_n[0:1, 64:128] = sendn_ref[1:2, :]
    index_p = rows_of(idx_p[...])
    index_n = rows_of(idx_n[...])

    out_p[...] = take(own, index_p)

    pl.semaphore_wait(barrier, len(greeted))
    up = send(out_p, in_p.at[0], p_upper)
    down = send(out_p, in_p.at[1], p_lower)
    mate = send(rec, rec_other, partner)
    started += [up, down, mate]

    embedding = split(
        jnp.concatenate([emb_ref[...], jnp.zeros((4, 128), F32)], axis=0)
    )
    mixed = mm(embedding, split(mix_ref[...]))
    selfed = mm(embedding, split(self_ref[...]))
    radial = radial_ref[...]
    weights = jnp.concatenate([radial * mixed[s : s + 1, :] for s in range(SPECIES)], axis=0)
    weights_all = split(jnp.concatenate([weights, selfed], axis=0))
    weights = (weights_all[0][0 : SPECIES * NB], weights_all[1][0 : SPECIES * NB])

    up.wait_recv()
    down.wait_recv()
    shift = (sub == 0).astype(F32) * (N_XY * width_x)
    from_lower = in_p[0] - jnp.where(xy == 0, shift, jnp.zeros_like(shift))
    from_upper = in_p[1] + jnp.where(xy == N_XY - 1, shift, jnp.zeros_like(shift))
    tile_1 = jnp.where(lane < 32, from_lower, from_upper)
    low = jnp.bitwise_and(index_n, 127)
    out_n[...] = jnp.where(index_n < OWN, take(own, low), take(tile_1, low))
    below = send(out_n, in_n.at[1], g_lower)
    above = send(out_n, in_n.at[0], g_upper)
    started += [below, above]

    mate.wait_recv()
    both = jnp.concatenate([own, rec_other[...]], axis=1)
    steps = iota((8, 2 * OWN), 0).astype(F32)

    def circle(turns):
        angle = (2.0 * jnp.pi) * (turns - jnp.floor(turns + 0.5))
        return jnp.cos(angle), jnp.sin(angle)

    cos_x, sin_x = circle(both[0:1, :] * (steps / (N_XY * width_x)))
    cos_y, sin_y = circle(both[1:2, :] * ((steps - KGRID // 2) / width_y))
    cos_z, sin_z = circle(
        both[2:3, :] * ((steps - KGRID // 2) / (N_GZ * width_z)) - 0.25 * core.astype(F32)
    )
    cos_z = cos_z * both[4:5, :]
    sin_z = sin_z * both[4:5, :]
    pairs = []
    for k in range(KGRID):
        cy, sy = cos_y[k : k + 1, :], sin_y[k : k + 1, :]
        pairs.append((cy * cos_z - sy * sin_z, sy * cos_z + cy * sin_z))
    wave_p = []
    for k in range(KGRID):
        cx, sx = cos_x[k : k + 1, :], sin_x[k : k + 1, :]
        for j in range(KGRID):
            c, s = pairs[j]
            wave_p.append(cx * c - sx * s)
            trig_q[k * KGRID + j] = -(sx * c + cx * s)
    wave_p = jnp.concatenate(wave_p, axis=0)

    below.wait_recv()
    above.wait_recv()
    pad_column = jnp.where(sub < 3, far_away, 0.0)
    zeros = jnp.zeros((8, OWN), F32)
    from_below = jnp.where(gz == 0, zeros, in_n[0])
    from_above = jnp.where(gz == N_GZ - 1, zeros, in_n[1])
    tile_1 = jnp.where(lane < 64, tile_1, from_below)
    tile_2 = jnp.where(lane < 64, from_above, pad_column)

    bases = iota((NB, OWN), 0).astype(F32)
    sums = [jnp.zeros((NB, OWN), F32) for _ in range(SPECIES)]
    for m in range(NEIGH):
        index = rows_of(neigh_ref[m : m + 1, :])
        low = jnp.bitwise_and(index, 127)
        found = jnp.where(
            index < OWN,
            take(own, low),
            jnp.where(index < 2 * OWN, take(tile_1, low), take(tile_2, low)),
        )
        offset = found - own
        square = offset * offset
        distance = jnp.sqrt(square[0:1] + square[1:2] + square[2:3] + softening)
        units[m] = jnp.where(sub < 3, offset / distance, 0.0)
        code = jnp.where(found[4:5] > 0.5, found[3:4], -1.0)
        codes[m : m + 1, :] = code
        ratio = distance / envelope_reach
        cube = ratio * ratio * ratio
        envelope = 1.0 / (1.0 + ratio * cube)
        scaled = distance / spacing - bases
        basis = jnp.exp(-scaled * scaled) * envelope
        slopes[m] = basis * ((-2.0 / spacing) * scaled - envelope * cube)
        for s in range(SPECIES):
            sums[s] = sums[s] + jnp.where(code == float(s), basis, 0.0)

    kind_row = own[3:4, :]
    hot_kind = (kind_row == sub.astype(F32)).astype(F32)
    mixing = jnp.concatenate(sums + [hot_kind], axis=0)
    before = mm(split(mixing.T), weights_all)
    gate = sigmoid(before)
    hidden = before * gate
    hidden_slope = gate * (1.0 + before * (1.0 - gate))
    hidden_2 = split(hidden)
    charge_w = split(charge_ref[...])
    charges = mm(hidden_2, charge_w)
    q_out[...] = charges
    mate_q = send(q_out, q_in, partner)
    started += [mate_q]

    readout_w = split(readout_ref[...])
    ahead = mm(hidden_2, readout_w)
    gate = sigmoid(ahead)
    live_column = (iota((OWN, 128), 0) < counts_ref[0]).astype(F32)
    vector = vector_ref[...]
    atom_row = jnp.sum(ahead * gate * live_column, axis=0, keepdims=True) * vector
    ahead_grad = live_column * vector * (gate * (1.0 + ahead * (1.0 - gate)))

    mate_q.wait_recv()
    q_both = jnp.concatenate([charges, q_in[...]], axis=0)
    q_pair = split(q_both)
    partial = mm(split(wave_p), q_pair)
    part[...] = partial.reshape(KGRID * KGRID, 8, 128)
    part[ZERO_TILE] = jnp.where(sub == ZERO_ROW, atom_row, part[ZERO_TILE])

    colours = ((0, z, z_peers, NZ, y, y_peers), (1, y, y_peers, NY, z, z_peers))
    phase = []
    for colour, me, peers, size, _, _ in colours:
        base = colour * HALF
        copies = []
        for d in range(1, size):
            start = base + CHUNK * lax.rem(me + d, size)
            copies.append(
                send(part.at[pl.ds(start, CHUNK)], gather_1.at[colour, d - 1], peers[d - 1])
            )
        phase.append(copies)
        started += copies

    hidden_grad = mm(split(ahead_grad), readout_w, NT)
    trig_t = split(wave_p.T)
    trig_pt[0] = trig_t[0]
    trig_pt[1] = trig_t[1]
    q_t = split(q_both.T)
    rows = iota((SLOTS, OWN), 0)
    for m in range(NEIGH):
        hot[:, m * OWN : (m + 1) * OWN] = (
            (neigh_ref[m : m + 1, :] == rows).astype(F32).astype(BF16)
        )

    swap = []
    for colour, me, peers, size, other, other_peers in colours:
        for copy in phase[colour]:
            copy.wait_recv()
        total = part[pl.ds(colour * HALF + CHUNK * me, CHUNK)]
        for d in range(1, size):
            total = total + gather_1[colour, d - 1]
        swap_2[colour, other] = total
        copies = [
            send(swap_2.at[colour, other], swap_2.at[colour, other], device)
            for device in other_peers
        ]
        swap.append(copies)
        started += copies
    last = []
    for colour, me, peers, size, other, other_peers in colours:
        for copy in swap[colour]:
            copy.wait_recv()
        total = swap_2[colour, 0]
        for d in range(1, NY):
            total = total + swap_2[colour, d]
        swap_3[colour, x] = total
        copies = [
            send(swap_3.at[colour, x], swap_3.at[colour, x], device) for device in x_peers
        ]
        last.append(copies)
        started += copies
    spread = []
    for colour, me, peers, size, other, other_peers in colours:
        for copy in last[colour]:
            copy.wait_recv()
        total = swap_3[colour, 0]
        for d in range(1, NX):
            total = total + swap_3[colour, d]
        place = pl.ds(colour * HALF + CHUNK * me, CHUNK)
        final[place] = total
        copies = [send(final.at[place], final.at[place], device) for device in peers]
        spread += copies
        started += copies
    for copy in spread:
        copy.wait_recv()

    keep = 1.0 - ((iota((64, 8, 128), 0) == ZERO_TILE) & (iota((64, 8, 128), 1) == ZERO_ROW)).astype(F32)
    structure = final[...]
    wave_weight = keep * filter_ref[...] * structure / ATOMS
    ewald = 0.5 * jnp.sum(wave_weight * structure, axis=0)
    ewald = ewald + jnp.where(sub == ZERO_ROW, final[ZERO_TILE], 0.0)
    ewald = jnp.sum(ewald, axis=0, keepdims=True)
    weight_2 = split(wave_weight.reshape(512, 128))
    charge_grad = mm((trig_pt[0], trig_pt[1]), weight_2)
    along = mm(weight_2, q_t).reshape(KGRID, KGRID, 8, 2 * OWN)
    phase_grad = along * trig_q[...].reshape(KGRID, KGRID, 8, 2 * OWN)
    by_x = jnp.sum(phase_grad, axis=1)
    by_y = jnp.sum(phase_grad, axis=0)
    along_x = sum(float(k) * by_x[k] for k in range(1, KGRID))
    along_y = sum(float(k - KGRID // 2) * by_y[k] for k in range(KGRID) if k != KGRID // 2)
    along_z = jnp.sum(by_y, axis=0) * (steps - KGRID // 2)

    def down_rows(value, factor):
        return jnp.sum(value, axis=0, keepdims=True) * (2.0 * jnp.pi * factor)

    wave_grad = jnp.concatenate(
        [
            down_rows(along_x, 1.0 / (N_XY * width_x)),
            down_rows(along_y, 1.0 / width_y),
            down_rows(along_z, 1.0 / (N_GZ * width_z)),
            jnp.zeros((5, 2 * OWN), F32),
        ],
        axis=0,
    )
    grad_out[...] = charge_grad[OWN:, :]
    misc_out[0] = wave_grad[:, OWN:]
    misc_out[1] = rows_of(ewald)
    mate_g = send(grad_out, grad_in, partner)
    mate_m = send(misc_out, misc_in, partner)
    started += [mate_g, mate_m]
    mate_g.wait_recv()
    mate_m.wait_recv()
    charge_grad = charge_grad[0:OWN, :] + grad_in[...]
    wave_grad = wave_grad[:, 0:OWN] + misc_in[0]
    energy = jnp.sum(ewald + misc_in[1, 0:1, :], axis=1, keepdims=True)
    energy_out[...] = energy / ATOMS

    hidden_grad = hidden_grad + mm(split(charge_grad), charge_w, NT)
    before_grad = hidden_grad * hidden_slope
    mixing_grad = mm(weights, split(before_grad), NT)
    pulls = [mixing_grad[s * NB : (s + 1) * NB, :] for s in range(SPECIES)]
    own_grad = jnp.zeros((8, OWN), F32)
    spread_sum = jnp.zeros((16, SLOTS), F32)
    columns = []
    for m in range(NEIGH):
        code = codes[m : m + 1, :]
        pull = jnp.where(code == 0.0, pulls[0], 0.0)
        for s in range(1, SPECIES):
            pull = jnp.where(code == float(s), pulls[s], pull)
        along_pair = jnp.sum(pull * slopes[m], axis=0, keepdims=True)
        push = units[m] * along_pair
        own_grad = own_grad - push
        high, small = split(push)
        columns.append(jnp.concatenate([high, small], axis=0))
    columns = jnp.concatenate(columns, axis=1)
    spread_sum = lax.dot_general(columns, hot[...], NT, preferred_element_type=F32)
    spread_sum = spread_sum[0:8] + spread_sum[8:16]

    back_n_out[0] = spread_sum[:, OWN : 2 * OWN]
    back_n_out[1] = spread_sum[:, 2 * OWN :]
    to_below = send(back_n_out.at[0], back_n_in.at[0], g_lower)
    to_above = send(back_n_out.at[1], back_n_in.at[1], g_upper)
    started += [to_below, to_above]
    hot_n = (iota((2 * OWN, OWN), 0) == idx_n[...]).astype(F32).astype(BF16)
    hot_p = ((iota((OWN, OWN), 0) == idx_p[...]) & (iota((OWN, OWN), 1) < 64)).astype(F32).astype(BF16)
    to_below.wait_recv()
    to_above.wait_recv()
    came = jnp.where(
        lane < 64,
        jnp.where(gz == 0, zeros, back_n_in[1]),
        jnp.where(gz == N_GZ - 1, zeros, back_n_in[0]),
    )

    def scatter(value, table):
        high, small = split(value)
        both = lax.dot_general(
            jnp.concatenate([high, small], axis=0), table, NT, preferred_element_type=F32
        )
        return both[0:8] + both[8:16]

    section = spread_sum[:, 0 : 2 * OWN] + scatter(came, hot_n)
    back_p_out[...] = section[:, OWN:]
    to_lower = send(back_p_out, back_p_in.at[0], p_lower)
    to_upper = send(back_p_out, back_p_in.at[1], p_upper)
    started += [to_lower, to_upper]
    own_grad = own_grad + section[:, 0:OWN] + wave_grad
    to_lower.wait_recv()
    to_upper.wait_recv()
    came = jnp.where(lane < 32, back_p_in[0], jnp.where(lane < 64, back_p_in[1], zeros))
    own_grad = own_grad + scatter(came, hot_p)
    forces_new = -own_grad[0:3, :]
    force_out[...] = forces_new
    vel_out[...] = half_velocity + (0.5 * time_step) * forces_new * mass_row

    for copy in started:
        copy.wait_send()


COPIES = 11 + 2 * (2 * 7 + 7 + 3)


def local(
    positions,
    velocities,
    forces,
    species,
    counts,
    neighbours,
    send_inplane,
    send_normal,
    embedding,
    inverse_mass,
    radial_weight,
    mix_weight,
    self_weight,
    charge_weight,
    readout_weight,
    readout_vector,
    kernel_filter,
):
    vmem = pl.BlockSpec(memory_space=pltpu.VMEM)
    smem = pl.BlockSpec(memory_space=pltpu.SMEM)
    tile = (8, 128)
    out = pl.pallas_call(
        kernel,
        out_shape=(
            jax.ShapeDtypeStruct((3, OWN), F32),
            jax.ShapeDtypeStruct((3, OWN), F32),
            jax.ShapeDtypeStruct((3, OWN), F32),
            jax.ShapeDtypeStruct((1, 1), F32),
        ),
        in_specs=[smem, smem] + [vmem] * 15,
        out_specs=(vmem, vmem, vmem, vmem),
        scratch_shapes=[
            pltpu.VMEM(tile, F32),
            pltpu.VMEM(tile, F32),
            pltpu.VMEM((1, 128), jnp.int32),
            pltpu.VMEM((1, 128), jnp.int32),
            pltpu.VMEM(tile, F32),
            pltpu.VMEM((2, 8, 128), F32),
            pltpu.VMEM(tile, F32),
            pltpu.VMEM((2, 8, 128), F32),
            pltpu.VMEM((128, 128), F32),
            pltpu.VMEM((128, 128), F32),
            pltpu.VMEM((64, 8, 128), F32),
            pltpu.VMEM((2, 7, CHUNK, 8, 128), F32),
            pltpu.VMEM((2, 8, CHUNK, 8, 128), F32),
            pltpu.VMEM((2, 4, CHUNK, 8, 128), F32),
            pltpu.VMEM((64, 8, 128), F32),
            pltpu.VMEM((128, 128), F32),
            pltpu.VMEM((128, 128), F32),
            pltpu.VMEM((2, 8, 128), F32),
            pltpu.VMEM((2, 8, 128), F32),
            pltpu.VMEM((2, 8, 128), F32),
            pltpu.VMEM((2, 8, 128), F32),
            pltpu.VMEM(tile, F32),
            pltpu.VMEM((2, 8, 128), F32),
            pltpu.VMEM((NEIGH, NB, 128), F32),
            pltpu.VMEM((NEIGH, 8, 128), F32),
            pltpu.VMEM((NEIGH, 128), F32),
            pltpu.VMEM((64, 8, 256), F32),
            pltpu.VMEM((2, 256, 512), BF16),
            pltpu.VMEM((SLOTS, NEIGH * OWN), BF16),
            pltpu.SemaphoreType.DMA((COPIES + 8,)),
            pltpu.SemaphoreType.DMA((COPIES + 8,)),
        ],
        compiler_params=pltpu.CompilerParams(
            collective_id=0, has_side_effects=True
        ),
    )(
        counts,
        inverse_mass,
        positions,
        velocities,
        forces,
        species.reshape(1, OWN),
        neighbours,
        send_inplane,
        send_normal,
        embedding,
        radial_weight,
        mix_weight,
        self_weight,
        charge_weight,
        readout_weight,
        readout_vector.reshape(1, 128),
        kernel_filter.reshape(64, 8, 128),
    )
    return out[0], out[1], out[2], out[3].reshape(())


def solution(mesh):
    return jax.shard_map(
        local,
        mesh=mesh,
        in_specs=(
            P(None, ("gz", "xy")),
            P(None, ("gz", "xy")),
            P(None, ("gz", "xy")),
            P(("gz", "xy")),
            P(("gz", "xy")),
            P(None, ("gz", "xy")),
            P(None, ("gz", "xy")),
            P(None, ("gz", "xy")),
            P(),
            P(),
            P(),
            P(),
            P(),
            P(),
            P(),
            P(),
            P(),
        ),
        out_specs=(P(None, ("gz", "xy")), P(None, ("gz", "xy")), P(None, ("gz", "xy")), P()),
        check_vma=False,
    )
```

time: 402 us -> 61.1 us (0.15)
  waiting for transfers between devices: 173 us -> 0 us
  blocking collectives: 104 us -> 0 us
  Pallas kernels: 0 us -> 55.1 us
  other arithmetic: 33.5 us -> 0 us
  starting transfers between devices: 31.2 us -> 0 us
  local copies, waits for them, and re-layouts: 26.5 us -> 2.57 us
  matrix products: 16.2 us -> 0 us
  between operations: 17.7 us -> 3.12 us
    psum x1 -> x0, waiting for transfers between devices: 171 us -> none  [local(): cosine_sum, sine_sum = lax.psum((cosine_sum, sine_sum), ('gz', 'xy'))]
    psum x1 -> x0, blocking collectives: 104 us -> none  [local(): local_total = lax.psum(local_sum, ('gz', 'xy'))]
    pallas_call x0 -> x1, Pallas kernels: none -> 55.1 us  [local(): pl.pallas_call(kernel, out_shape=(jax.ShapeDtypeStruct((3, OWN), F32), ja...]
    ppermute x8 -> x0, starting transfers between devices: 31.2 us -> none  [the longest x4 20.3 us: padded(): lax.ppermute(head, axis, [((i + 1) % count, i) for i in range(ends)])]
    gather x6 -> x0, local copies, waits for them, and re-layouts: 21.3 us -> none  [the longest x1 10.8 us: local_terms(): gathered = jnp.take(outgoing, neighbour_rows, axis=0)]
    scatter-add x5 -> x0, other arithmetic: 21.2 us -> none  [the longest x1 17.7 us: local_terms(): partner = jnp.take(ext_pos, neighbour_rows, axis=1)]
    dot_general x18 -> x0, matrix products: 16.2 us -> none  [the longest x2 5.14 us: local_terms(): jnp.einsum('bma,bc->mac', radial_basis, radial_weight, precision=highest)]
    reduce_sum x4 -> x0, other arithmetic: 5.05 us -> none  [the longest x1 2.42 us: local_terms(): offsets = partner - centre[:, None, :]]
  transfers between devices with their start and end apart: 9 -> 0, of which waited for: 4 -> 0; matrix products, arithmetic and copies ran while one was open for 3% -> 0% of each run, Pallas kernels for 0% -> 0%
where the time goes in v1:
time: 61.1 us; the launch traced here: 60.8 us
  Pallas kernels  55.1 us (90%)
  between operations  3.12 us (5%)
  local copies, waits for them, and re-layouts  2.57 us (4%)
    pallas_call x1, Pallas kernels, local(): pl.pallas_call(kernel, out_shape=(jax.ShapeDtypeStruct((3, OWN), F32), ja...  55.1 us
    unnamed x9, local copies, waits for them, and re-layouts  2.57 us

profile of v1, /device:TPU:1, one launch (start us, length us, event | category | flops | bytes accessed | tf_op | source)
XLA Modules:
  0.0 60.8 jit_solution(686447096943418497)
XLA Ops:
  1.3 55.1 %shard_map.192 = (f32[3,128]{1,0:T(4,128)}, f32[3,128]{1,0:T(4,128)}, f32[3,128]{1,0:T(4,128)}, f32[1,1]{1,0:T(1,128)}) custom-call(s32[1]{0:T(128)S(6)} %copy.25.counts_ref, f32[4]{0:T(128)} %mass_ref.1, f32[3,128]{1,0:T(4,128)} %pos_ref.1, f32[3,128]{1,0:T(4,128)} %vel_ref.1, f32[3,128]{1,0:T(4,128)} %force_ref.1, s32[1,128]{1,0:T(1,128)} %bitcast.5, ...), custom_call_target="tpu_custom_call" | custom-call | tf_op jit(solution)/shard_map/pallas_call | solution.py:503
  56.4 0.0 copy-start.2
  56.4 0.6 %copy-done.2 = f32[3,128]{1,0:T(4,128)S(1)} copy-done((f32[3,128]{1,0:T(4,128)S(1)}, f32[3,128]{1,0:T(4,128)}, u32[]{:S(2)}) %copy-start.2) | copy-done | bytes 1560
  57.1 0.0 copy-start.1
  57.1 0.6 copy.26
  57.7 0.1 copy-done.1
  57.8 0.0 copy-start
  57.8 0.6 copy.27
  58.3 0.1 copy-done
  58.4 0.6 copy.28
Async XLA Ops:
  56.4 0.7 %copy-start.2 = (f32[3,128]{1,0:T(4,128)S(1)}, f32[3,128]{1,0:T(4,128)}, u32[]{:S(2)}) copy-start(f32[3,128]{1,0:T(4,128)} %get-tuple-element.16) | copy-start | bytes 4612
  57.1 0.7 %copy-start.1 = (f32[3,128]{1,0:T(4,128)S(1)}, f32[3,128]{1,0:T(4,128)}, u32[]{:S(2)}) copy-start(f32[3,128]{1,0:T(4,128)} %get-tuple-element.17) | copy-start | bytes 4612
  57.8 0.7 %copy-start = (f32[3,128]{1,0:T(4,128)S(1)}, f32[3,128]{1,0:T(4,128)}, u32[]{:S(2)}) copy-start(f32[3,128]{1,0:T(4,128)} %get-tuple-element.18) | copy-start | bytes 4612
